TPU v7x, 512 devices: a whole 4x8x8 slice. The times are simulated.
512 devices in a mesh: bank: 8 (over x, core), gal: 64 (over z, y).
Axes of the slice: x: 4, y: 8, z: 8, core: 2. Of those that a mesh axis runs over, the one named last changes fastest.
Arguments:
- bank_queries: bfloat16 [4096, 768], P(('bank', 'gal'))
- gallery: bfloat16 [262144, 768], P('gal')
- test_queries: bfloat16 [2048, 768], P(('bank', 'gal'))
- test_slabs: int32 [2048, 8], P('bank'), may hold values from 0 to 63, all different within a row; in each aligned block of 4 rows (0 to 3, 4 to 7, ...) at most 2 rows name the same one
- test_offsets: int32 [2048, 8], P('bank'), may hold values from 0 to 31
Outputs:
- pooled: float32 [2048, 768], P(('bank', 'gal'))
Inputs may be any that keep to these rules, and one draw needn't show every extreme that they name: `test_slabs`: each row names 8 different slabs; the 4 rows of one device name no slab more than 2 times, and on some devices one slab exactly 2 times.
All inputs are finite; a program needn't handle non-finite values.
Results may differ from a plain program's by a relative error of at most 0.0065.
Values may be sent and summed in bfloat16 or wider, within the bound.
A program may use at most 64 MiB of HBM per device.

v0:
```python
import jax
import jax.numpy as jnp
from jax import lax
from jax.sharding import PartitionSpec as P

BLOCK = 128


SHARPNESS = 20.0
epsilon = 1e-06


def row_scale(matrix):
    values = matrix.astype(jnp.float32)
    return lax.rsqrt(jnp.sum(values * values, axis=1) + epsilon)


def inner_rows(first_rows, second_rows):
    return lax.dot_general(
        first_rows, second_rows, (((1,), (1,)), ((), ())), preferred_element_type=jnp.float32
    )


def body(bank_queries, gallery, test_queries, test_slabs, test_offsets):
    gallery_rows = gallery.shape[0]
    gallery_scale = row_scale(gallery)
    portion = lax.all_gather(bank_queries, "gal", axis=0, tiled=True)
    scores = (
        SHARPNESS
        * inner_rows(portion, gallery)
        * row_scale(portion)[:, None]
        * gallery_scale[None, :]
    )
    partial_sums = jnp.sum(jnp.exp(scores), axis=0)
    colsum = lax.psum(partial_sums, "bank")
    log_col = jnp.log(colsum)
    own_rows = test_queries.shape[0]
    slab_index = lax.axis_index("gal")
    queries = lax.all_gather(test_queries, "gal", axis=0, tiled=True)
    blocks_here = gallery_rows // BLOCK
    local_blocks = jnp.arange(blocks_here, dtype=jnp.int32)
    block_hits = (test_slabs == slab_index)[:, :, None] & (
        test_offsets[:, :, None] == local_blocks[None, None, :]
    )
    listed = jnp.any(block_hits, axis=1)
    row_mask = jnp.repeat(listed, BLOCK, axis=1)
    logits = (
        SHARPNESS
        * inner_rows(queries, gallery)
        * row_scale(queries)[:, None]
        * gallery_scale[None, :]
        - log_col[None, :]
    )
    weights = jnp.where(row_mask, jnp.exp(logits), jnp.float32(0.0))
    numerator = jnp.dot(weights.astype(jnp.bfloat16), gallery, preferred_element_type=jnp.float32)
    numerator, denominator = (numerator, jnp.sum(weights, axis=1))
    numer_all, denom_all = lax.psum((numerator, denominator), "gal")
    offset = slab_index * own_rows
    numer_own = lax.dynamic_slice_in_dim(numer_all, offset, own_rows, 0)
    denom_own = lax.dynamic_slice_in_dim(denom_all, offset, own_rows, 0)
    return numer_own / denom_own[:, None]


def solution(mesh):
    in_specs = (
        P(("bank", "gal"), None),
        P("gal", None),
        P(("bank", "gal"), None),
        P("bank", None),
        P("bank", None),
    )
    out_specs = P(("bank", "gal"), None)
    return jax.shard_map(body, mesh=mesh, in_specs=in_specs, out_specs=out_specs, check_vma=False)
```

profile of v0, /device:TPU:1, one launch (start us, length us, event | category | flops | bytes accessed | tf_op | source)
XLA Modules:
  0.0 314.7 jit_solution(15684312714763030671)
XLA Ops:
  6.5 0.0 copy-start.1
  6.5 0.0 copy-start.2
  6.5 0.0 copy-start.3
  6.5 0.0 copy-start
  6.5 0.0 all-reduce.2.cloned.1.call-start
  6.6 4.1 %multiply_reduce_fusion = f32[4096]{0:T(1024)S(1)} fusion(bf16[4096,768]{1,0:T(8,128)(2,1)} %param.6), kind=kLoop, calls=%fused_computation | loop fusion | flops 9433088 | bytes 6307840 | tf_op jit(solution)/shard_map/reduce_sum | solution.py:15
  10.7 0.0 copy-done.1
  10.7 0.0 copy-done.2
  10.8 0.1 copy.10
  10.9 0.0 copy-done.3
  10.9 45.1 %all-gather = bf16[64,4,768]{2,1,0:T(4,128)(2,1)S(1)} all-gather(bf16[1,4,768]{2,1,0:T(4,128)(2,1)S(1)} %bitcast.13), channel_id=1, replica_groups=mesh['bank'=8,'gal'=64] {'gal'}, dimensions={0}, use_global_device_ids=true | all-gather | bytes 399360 | tf_op jit(solution)/shard_map/all_gather | solution.py:39
  56.1 0.1 reshape.21
  56.2 0.2 multiply_reduce_fusion.2
  56.3 0.0 copy-done
  56.3 37.0 %all_gather.7 = bf16[512,768]{1,0:T(8,128)(2,1)S(1)} all-gather(bf16[8,768]{1,0:T(8,128)(2,1)S(1)} %copy-done), channel_id=1, replica_groups=mesh['bank'=8,'gal'=64] {'gal'}, dimensions={0}, use_global_device_ids=true | all-gather | bytes 798720 | tf_op jit(solution)/shard_map/all_gather | solution.py:27
  93.4 0.2 multiply_reduce_fusion.1
  93.6 6.5 %exponential_reduce_fusion = f32[4096]{0:T(1024)S(1)} fusion(bf16[512,768]{1,0:T(8,128)(2,1)S(1)} %all_gather.7, bf16[4096,768]{1,0:T(8,128)(2,1)} %param.6, f32[4096]{0:T(1024)S(1)} %add_rsqrt_fusion, f32[512]{0:T(512)S(1)} %rsqrt_multiply_fusion), kind=kOutput, calls=%fused_computation.1 | convolution fusion | flops 3227512832 | bytes 7112704 | tf_op jit(solution)/shard_map/dot_general | solution.py:19
  100.2 44.7 %psum.21 = f32[4096]{0:T(1024)S(1)} all-reduce(f32[4096]{0:T(1024)S(1)} %exponential_reduce_fusion), channel_id=1, replica_groups=mesh['bank'=8,'gal'=64] {'bank'}, use_global_device_ids=true, to_apply=%region_5.0 | all-reduce | flops 4096 | bytes 32768 | tf_op jit(solution)/shard_map/psum | solution.py:35
  144.8 0.0 slice-start
  144.8 2.1 broadcast_in_dim.5
  146.9 0.0 slice-start.1
  146.9 5.3 %fusion.8 = (f32[256]{0:T(256)S(1)}, bf16[256,4096]{1,0:T(8,128)(2,1)S(1)}) fusion(f32[4096]{0:T(1024)S(1)} %log.3, f32[4096]{0:T(1024)S(1)} %add_rsqrt_fusion, f32[256]{0:T(256)S(1)} %rsqrt_multiply_fusion.1, bf16[256,768]{1,0:T(8,128)(2,1)S(1)} %reshape.21, bf16[4096,768]{1,0:T(8,128)(2,1)} %param.6, pred[32,8,32,128]{3,2,1,0:T(32,128)(4,1)S(1)} %bitcast.12), kind=kOutput, calls=%fused_computation.19 | convolution fusion | flops 1616903936 | bytes 9865216 | tf_op jit(solution)/shard_map/dot_general | solution.py:19
  152.2 0.0 slice-done
  152.2 0.0 slice-done.1
  152.3 2.7 fusion.4
  155.0 0.0 all-reduce.2.cloned.1.call-update
  155.0 113.1 %psum.23 = f32[256]{0:T(256)S(1)} all-reduce(f32[256]{0:T(256)S(1)} %get-tuple-element.5), channel_id=1, replica_groups=mesh['bank'=8,'gal'=64] {'gal'}, use_global_device_ids=true, to_apply=%region_8.9 | all-reduce | flops 256 | bytes 2048 | tf_op jit(solution)/shard_map/psum | solution.py:57
  268.1 0.1 dynamic_slice.7
  268.2 38.2 %all-reduce.2.cloned.1.call-done = f32[256,768]{1,0:T(8,128)} async-done(((f32[256,768]{1,0:T(8,128)}), f32[256,768]{1,0:T(8,128)}) %all-reduce.2.cloned.1.call-update) | async-done | bytes 786448 | tf_op jit(solution)/shard_map/psum | solution.py:57
  306.4 1.4 dynamic-slice_divide_fusion
  (7 shorter events, 0.1 us)
Async XLA Ops:
  6.5 4.2 %copy-start.1 = (s32[256,8]{0,1:T(8,128)S(1)}, s32[256,8]{0,1:T(8,128)}, u32[]{:S(2)}) copy-start(s32[256,8]{0,1:T(8,128)} %param.8) | copy-start | bytes 24580
  6.5 4.2 %copy-start.2 = (s32[256,8]{0,1:T(8,128)S(1)}, s32[256,8]{0,1:T(8,128)}, u32[]{:S(2)}) copy-start(s32[256,8]{0,1:T(8,128)} %param.9) | copy-start | bytes 24580
  6.5 4.4 %copy-start.3 = (bf16[4,768]{1,0:T(4,128)(2,1)S(1)}, bf16[4,768]{1,0:T(4,128)(2,1)}, u32[]{:S(2)}) copy-start(bf16[4,768]{1,0:T(4,128)(2,1)} %param.7) | copy-start | bytes 18436
  6.5 49.8 %copy-start = (bf16[8,768]{1,0:T(8,128)(2,1)S(1)}, bf16[8,768]{1,0:T(8,128)(2,1)}, u32[]{:S(2)}) copy-start(bf16[8,768]{1,0:T(8,128)(2,1)} %param.5) | copy-start | bytes 36868
  6.5 299.9 %all-reduce.2.cloned.1.call-start = ((), (), s32[]{:S(2)}) async-start(), calls=%async_computation | async-start | bytes 1572864 | tf_op jit(solution)/shard_map/psum | solution.py:57
  144.8 7.4 %slice-start = ((s8[6291456]{0:T(1024)(128)(4,1)}), s8[4194304]{0:T(1024)(128)(4,1)S(1)}, s32[]{:S(2)}) async-start(s8[6291456]{0:T(1024)(128)(4,1)} %bitcast.10), calls=%async_computation.1 | async-start | bytes 8388608
  146.9 5.3 %slice-start.1 = ((s8[6291456]{0:T(1024)(128)(4,1)}), s8[2097152]{0:T(1024)(128)(4,1)S(1)}, s32[]{:S(2)}) async-start(s8[6291456]{0:T(1024)(128)(4,1)} %bitcast.10), calls=%async_computation.2 | async-start | bytes 4194304
Sparse Core Ops, SparseCore 0:
  155.1 151.2 all-reduce.1
where the time goes:
time: 318 us; the launch traced here: 315 us
  blocking collectives  240 us (75%)
  waiting for transfers between devices  38.2 us (12%)
  matrix products  14.5 us (5%)
  between operations  13.5 us (4%)
  other arithmetic  5.96 us (2%)
    psum x1, blocking collectives, body(): numer_all, denom_all = lax.psum((numerator, denominator), 'gal')  113 us
    all_gather x1, blocking collectives, body(): queries = lax.all_gather(test_queries, 'gal', axis=0, tiled=True)  45.1 us
    psum x1, blocking collectives, body(): colsum = lax.psum(partial_sums, 'bank')  44.7 us
    psum x1, waiting for transfers between devices, body(): numer_all, denom_all = lax.psum((numerator, denominator), 'gal')  38.2 us
    all_gather x1, blocking collectives, body(): portion = lax.all_gather(bank_queries, 'gal', axis=0, tiled=True)  37 us
    dot_general x2, matrix products, inner_rows(): lax.dot_general(first_rows, second_rows, (((1,), (1,)), ((), ())), prefer...  11.8 us
  transfers between devices with their start and end apart: 1, of which 1 were waited for; matrix products, arithmetic and copies ran while one was open for 0% of the time, Pallas kernels for 0%

commit v1 on v0

v1 whole, which is shorter than its diff:
```python
import functools
import jax
import jax.numpy as jnp
from jax import lax
from jax.experimental import pallas as pl
from jax.experimental.pallas import tpu as pltpu
from jax.sharding import PartitionSpec as P

BLOCK = 128
SLOTS = 2
EXTRA = 128
SHARPNESS = 20.0
LOG2E = 1.4426950408889634
epsilon = 1e-06
MESH = pl.DeviceIdType.MESH
NT = (((1,), (1,)), ((), ()))
NN = (((1,), (0,)), ((), ()))


def matmul(left, right, dims):
    return lax.dot_general(left, right, dims, preferred_element_type=jnp.float32)


def kernel(
    n_bank, n_z, n_y, chunk,
    bankq_ref, testq_ref, slabs_ref, offsets_ref, gal_hbm,
    out_ref,
    gal, bank_all, test_all, gscale, sums, scores, back_out, back_in,
    gal_sem, hop_send, hop_recv, sum_send, sum_recv, back_send, back_recv,
):
    n_gal = n_z * n_y
    rows, width = gal.shape
    half = width // 2
    chunks = rows // chunk
    me_b = lax.axis_index("bank")
    me_g = lax.axis_index("gal")
    me_z = me_g // n_y
    me_y = me_g % n_y

    def load(n):
        part = pl.ds(n * chunk, chunk)
        return pltpu.make_async_copy(gal_hbm.at[part], gal.at[part], gal_sem.at[n])

    for n in range(chunks):
        load(n).start()

    barrier = pltpu.get_barrier_semaphore()

    def greet_gal(k, carry):
        pl.semaphore_signal(
            barrier, inc=1, device_id={"gal": (me_g + k) % n_gal}, device_id_type=MESH
        )
        return carry

    def greet_bank(k, carry):
        pl.semaphore_signal(
            barrier, inc=1, device_id={"bank": (me_b + k) % n_bank}, device_id_type=MESH
        )
        return carry

    lax.fori_loop(1, n_gal, greet_gal, 0)
    lax.fori_loop(1, n_bank, greet_bank, 0)
    pl.semaphore_wait(barrier, n_gal + n_bank - 2)

    gathers = ((bankq_ref, bank_all), (testq_ref, test_all))
    left, right = pl.ds(0, half), pl.ds(half, half)

    def first(t, side, k):
        own, full = gathers[t]
        cols = (left, right)[side]
        if side == 0:
            peer = me_z * n_y + (me_y + k) % n_y
        else:
            peer = (me_z + k) % n_z * n_y + me_y
        return pltpu.make_async_remote_copy(
            src_ref=own.at[:, cols],
            dst_ref=full.at[me_z, me_y, :, cols],
            send_sem=hop_send.at[t, side, 0, k],
            recv_sem=hop_recv.at[t, side, 0, k],
            device_id={"gal": peer},
            device_id_type=MESH,
        )

    def second(t, side, k):
        full = gathers[t][1]
        if side == 0:
            peer = (me_z + k) % n_z * n_y + me_y
            part = full.at[me_z, :, :, left]
        else:
            peer = me_z * n_y + (me_y + k) % n_y
            part = full.at[:, me_y, :, right]
        return pltpu.make_async_remote_copy(
            src_ref=part,
            dst_ref=part,
            send_sem=hop_send.at[t, side, 1, k],
            recv_sem=hop_recv.at[t, side, 1, k],
            device_id={"gal": peer},
            device_id_type=MESH,
        )

    spans = ((n_y, n_z), (n_z, n_y))
    for t in range(2):
        for side in range(2):
            for k in range(1, spans[side][0]):
                first(t, side, k).start()
    bank_all[me_z, me_y] = bankq_ref[...]
    test_all[me_z, me_y] = testq_ref[...]

    ones = jnp.ones((8, width), jnp.bfloat16)

    def norms(n, carry):
        load(n).wait()
        part = pl.ds(pl.multiple_of(n * chunk, chunk), chunk)
        values = gal[part, :].astype(jnp.float32)
        squares = values * values
        high = squares.astype(jnp.bfloat16)
        low = (squares - high.astype(jnp.float32)).astype(jnp.bfloat16)
        total = matmul(ones, high, NT) + matmul(ones, low, NT)
        gscale[:, part] = lax.rsqrt(total[0:1] + epsilon)
        return carry

    lax.fori_loop(0, chunks, norms, 0)

    for t in range(2):
        for side in range(2):
            for k in range(1, spans[side][0]):
                first(t, side, k).wait_recv()
            for k in range(1, spans[side][1]):
                second(t, side, k).start()

    slots = SLOTS * n_gal
    own_rows = testq_ref.shape[0]
    queries = n_gal * own_rows
    slabs = slabs_ref[...]
    offsets = offsets_ref[...].astype(jnp.float32)
    named = slabs == me_g
    hit = jnp.sum(jnp.where(named, 1.0, 0.0), axis=0, keepdims=True)
    place = jnp.sum(jnp.where(named, offsets, 0.0), axis=0, keepdims=True)
    hit8 = jnp.broadcast_to(hit, (8, queries))
    lane = lax.broadcasted_iota(jnp.int32, (8, queries), 1) % own_rows
    rank8 = jnp.zeros((8, queries), jnp.float32)
    for k in range(1, own_rows):
        rank8 = rank8 + jnp.where(lane >= k, pltpu.roll(hit8, k, 1), 0.0)
    rank = rank8[0:1]
    slot_row = lax.broadcasted_iota(jnp.int32, (slots, queries), 0)
    query_col = lax.broadcasted_iota(jnp.int32, (slots, queries), 1)
    pick = jnp.where(
        (query_col // own_rows == slot_row // SLOTS)
        & (hit > 0.5)
        & (rank.astype(jnp.int32) == slot_row % SLOTS),
        1.0,
        0.0,
    )
    slot_hit = jnp.sum(pick, axis=1, keepdims=True)
    slot_place = jnp.sum(pick * place, axis=1, keepdims=True)
    slot_block = jnp.where(slot_hit > 0.5, slot_place, -1.0).astype(jnp.int32)

    for side in range(2):
        for k in range(1, spans[side][1]):
            second(0, side, k).wait_recv()
    portion = bank_all[...].reshape(n_gal * bankq_ref.shape[0], width)
    values = portion.astype(jnp.float32)
    bank_scale = (SHARPNESS * LOG2E) * lax.rsqrt(
        jnp.sum(values * values, axis=1, keepdims=True) + epsilon
    )

    def column_sums(n, carry):
        part = pl.ds(pl.multiple_of(n * chunk, chunk), chunk)
        s = matmul(portion, gal[part, :], NT)
        e = jnp.exp2(s * bank_scale * gscale[:, part])
        sums[me_b, :, part] = jnp.sum(e, axis=0, keepdims=True)
        return carry

    lax.fori_loop(0, chunks, column_sums, 0)

    def share(k):
        return pltpu.make_async_remote_copy(
            src_ref=sums.at[me_b],
            dst_ref=sums.at[me_b],
            send_sem=sum_send.at[k],
            recv_sem=sum_recv.at[k],
            device_id={"bank": (me_b + k) % n_bank},
            device_id_type=MESH,
        )

    for k in range(1, n_bank):
        share(k).start()

    for side in range(2):
        for k in range(1, spans[side][1]):
            second(1, side, k).wait_recv()
    asked = matmul(
        pick.astype(jnp.bfloat16), test_all[...].reshape(queries, width), NN
    )
    test_scale = (SHARPNESS * LOG2E) * lax.rsqrt(
        jnp.sum(asked * asked, axis=1, keepdims=True) + epsilon
    )
    asked = asked.astype(jnp.bfloat16)

    def raw_weights(n, carry):
        part = pl.ds(pl.multiple_of(n * chunk, chunk), chunk)
        s = matmul(asked, gal[part, :], NT)
        e = jnp.exp2(s * test_scale * gscale[:, part])
        block = n * (chunk // BLOCK) + (
            lax.broadcasted_iota(jnp.int32, (slots, chunk), 1) // BLOCK
        )
        scores[:, part] = jnp.where(block == slot_block, e, 0.0)
        return carry

    lax.fori_loop(0, chunks, raw_weights, 0)

    for k in range(1, n_bank):
        share(k).wait_recv()
    inverse = 1.0 / jnp.sum(sums[...], axis=0)

    weights = scores[...] * inverse
    total = jnp.sum(weights, axis=1, keepdims=True)
    numer = matmul(weights.astype(jnp.bfloat16), gal[...], NN)
    total_high = total.astype(jnp.bfloat16).astype(jnp.float32)
    lanes = lax.broadcasted_iota(jnp.int32, (slots, EXTRA), 1)
    extra = jnp.where(lanes == 0, total_high, jnp.where(lanes == 1, total - total_high, 0.0))
    message = jnp.concatenate([numer, extra], axis=1).astype(jnp.bfloat16)
    back_out[...] = message.reshape(n_gal, SLOTS, width + EXTRA)

    def give(k, carry):
        peer = (me_g + k) % n_gal
        pltpu.make_async_remote_copy(
            src_ref=back_out.at[peer],
            dst_ref=back_in.at[me_g],
            send_sem=back_send,
            recv_sem=back_recv,
            device_id={"gal": peer},
            device_id_type=MESH,
        ).start()
        return carry

    lax.fori_loop(1, n_gal, give, 0)
    back_in[me_g] = back_out[me_g]

    slab_of = lax.broadcasted_iota(jnp.int32, (slots, queries), 0) // SLOTS
    lists = jnp.zeros((slots, queries), jnp.float32)
    for s in range(slabs_ref.shape[0]):
        lists = lists + jnp.where(slabs[s : s + 1] == slab_of, 1.0, 0.0)
    own_row = lax.broadcasted_iota(jnp.int32, (8, queries), 0)
    own_col = lax.broadcasted_iota(jnp.int32, (8, queries), 1)
    mine = jnp.where(
        (own_col == me_g * own_rows + own_row) & (own_row < own_rows), 1.0, 0.0
    )
    mine_lists = matmul(mine.astype(jnp.bfloat16), lists.astype(jnp.bfloat16), NT)
    before = jnp.where(
        lax.broadcasted_iota(jnp.int32, (8, 8), 1) < lax.broadcasted_iota(jnp.int32, (8, 8), 0),
        1.0,
        0.0,
    )
    mine_rank = matmul(before, mine_lists, NN)
    slot_col = lax.broadcasted_iota(jnp.int32, (8, slots), 1)
    take = jnp.where(
        (mine_lists > 0.5) & ((mine_rank + 0.5).astype(jnp.int32) == slot_col % SLOTS), 1.0, 0.0
    )

    everyone = pltpu.make_async_remote_copy(
        src_ref=back_out.at[pl.ds(0, n_gal - 1)],
        dst_ref=back_in.at[pl.ds(0, n_gal - 1)],
        send_sem=back_send,
        recv_sem=back_recv,
        device_id={"gal": (me_g + 1) % n_gal},
        device_id_type=MESH,
    )
    everyone.wait_recv()
    got = back_in[...].reshape(slots, width + EXTRA)
    answer = matmul(take.astype(jnp.bfloat16), got, NN)
    bottom = answer[:, width : width + 1] + answer[:, width + 1 : width + 2]
    out_ref[...] = (answer[:, :width] / bottom)[:own_rows]

    everyone.wait_send()
    for k in range(1, n_bank):
        share(k).wait_send()
    for t in range(2):
        for side in range(2):
            for k in range(1, spans[side][0]):
                first(t, side, k).wait_send()
            for k in range(1, spans[side][1]):
                second(t, side, k).wait_send()


def body(n_bank, n_z, n_y, chunk, bank_queries, gallery, test_queries, test_slabs, test_offsets):
    rows, width = gallery.shape
    n_gal = n_z * n_y
    own_bank, own_test = bank_queries.shape[0], test_queries.shape[0]
    slots = SLOTS * n_gal
    hops = (2, 2, 2, max(n_z, n_y))
    vmem = pl.BlockSpec(memory_space=pltpu.VMEM)
    return pl.pallas_call(
        functools.partial(kernel, n_bank, n_z, n_y, chunk),
        out_shape=jax.ShapeDtypeStruct((own_test, width), jnp.float32),
        in_specs=[vmem] * 4 + [pl.BlockSpec(memory_space=pl.ANY)],
        out_specs=vmem,
        scratch_shapes=[
            pltpu.VMEM((rows, width), jnp.bfloat16),
            pltpu.VMEM((n_z, n_y, own_bank, width), jnp.bfloat16),
            pltpu.VMEM((n_z, n_y, own_test, width), jnp.bfloat16),
            pltpu.VMEM((1, rows), jnp.float32),
            pltpu.VMEM((n_bank, 1, rows), jnp.float32),
            pltpu.VMEM((slots, rows), jnp.float32),
            pltpu.VMEM((n_gal, SLOTS, width + EXTRA), jnp.bfloat16),
            pltpu.VMEM((n_gal, SLOTS, width + EXTRA), jnp.bfloat16),
            pltpu.SemaphoreType.DMA((rows // chunk,)),
            pltpu.SemaphoreType.DMA(hops),
            pltpu.SemaphoreType.DMA(hops),
            pltpu.SemaphoreType.DMA((n_bank,)),
            pltpu.SemaphoreType.DMA((n_bank,)),
            pltpu.SemaphoreType.DMA,
            pltpu.SemaphoreType.DMA,
        ],
        compiler_params=pltpu.CompilerParams(
            collective_id=0, has_side_effects=True, vmem_limit_bytes=48 * 1024 * 1024
        ),
    )(bank_queries, test_queries, test_slabs.T, test_offsets.T, gallery)


def solution(mesh):
    n_bank, n_gal = mesh.shape["bank"], mesh.shape["gal"]
    n_z = 8 if n_gal == 64 else 2
    run = functools.partial(body, n_bank, n_z, n_gal // n_z, 512)
    in_specs = (
        P(("bank", "gal"), None),
        P("gal", None),
        P(("bank", "gal"), None),
        P("bank", None),
        P("bank", None),
    )
    out_specs = P(("bank", "gal"), None)
    return jax.shard_map(run, mesh=mesh, in_specs=in_specs, out_specs=out_specs, check_vma=False)
```

time: 318 us -> 61.9 us (0.19)
  blocking collectives: 240 us -> 0 us
  Pallas kernels: 0 us -> 58.1 us
  waiting for transfers between devices: 38.2 us -> 0 us
  matrix products: 14.5 us -> 0 us
  between operations: 13.5 us -> 0.01 us
  other arithmetic: 5.96 us -> 0 us
    psum x2 -> x0, blocking collectives: 158 us -> none  [the longest x1 113 us: body(): numer_all, denom_all = lax.psum((numerator, denominator), 'gal')]
    all_gather x2 -> x0, blocking collectives: 82.2 us -> none  [the longest x1 45.1 us: body(): queries = lax.all_gather(test_queries, 'gal', axis=0, tiled=True)]
    pallas_call x0 -> x1, Pallas kernels: none -> 58.1 us  [body(): pl.pallas_call(functools.partial(kernel, n_bank, n_z, n_y, chunk), out_sh...]
    psum x1 -> x0, waiting for transfers between devices: 38.2 us -> none  [body(): numer_all, denom_all = lax.psum((numerator, denominator), 'gal')]
    dot_general x3 -> x0, matrix products: 14.5 us -> none  [the longest x2 11.8 us: inner_rows(): lax.dot_general(first_rows, second_rows, (((1,), (1,)), ((), ())), prefer...]
    reduce_sum x3 -> x0, other arithmetic: 4.48 us -> none  [row_scale(): return lax.rsqrt(jnp.sum(values * values, axis=1) + epsilon)]
    unnamed x13 -> x9, local copies, waits for them, and re-layouts: 0.12 us -> 3.39 us
  transfers between devices with their start and end apart: 1 -> 0, of which waited for: 1 -> 0; matrix products, arithmetic and copies ran while one was open for 0% -> 0% of each run, Pallas kernels for 0% -> 0%
where the time goes in v1:
time: 61.9 us; the launch traced here: 61.5 us
  Pallas kernels  58.1 us (94%)
  local copies, waits for them, and re-layouts  3.39 us (5%)
    pallas_call x1, Pallas kernels, body(): pl.pallas_call(functools.partial(kernel, n_bank, n_z, n_y, chunk), out_sh...  58.1 us
    unnamed x9, local copies, waits for them, and re-layouts  3.39 us

profile of v1, /device:TPU:1, one launch (start us, length us, event | category | flops | bytes accessed | tf_op | source)
XLA Modules:
  0.0 61.5 jit_solution(16207692154604191834)
XLA Ops:
  0.0 0.0 copy-start
  0.0 0.7 %copy-done = bf16[8,768]{1,0:T(8,128)(2,1)S(1)} copy-done((bf16[8,768]{1,0:T(8,128)(2,1)S(1)}, bf16[8,768]{1,0:T(8,128)(2,1)}, u32[]{:S(2)}) %copy-start) | copy-done | bytes 12312
  0.7 0.0 copy-start.1
  0.7 0.7 %copy-done.1 = s32[256,8]{0,1:T(8,128)S(1)} copy-done((s32[256,8]{0,1:T(8,128)S(1)}, s32[256,8]{0,1:T(8,128)}, u32[]{:S(2)}) %copy-start.1) | copy-done | bytes 8216
  1.4 0.0 copy-start.2
  1.4 0.7 %copy-done.2 = s32[256,8]{0,1:T(8,128)S(1)} copy-done((s32[256,8]{0,1:T(8,128)S(1)}, s32[256,8]{0,1:T(8,128)}, u32[]{:S(2)}) %copy-start.2) | copy-done | bytes 8216
  2.1 0.0 copy-start.3
  2.1 0.7 %copy-done.3 = bf16[4,768]{1,0:T(4,128)(2,1)S(1)} copy-done((bf16[4,768]{1,0:T(4,128)(2,1)S(1)}, bf16[4,768]{1,0:T(4,128)(2,1)}, u32[]{:S(2)}) %copy-start.3) | copy-done | bytes 6168
  2.8 58.1 %shard_map.55 = f32[4,768]{1,0:T(4,128)S(1)} custom-call(bf16[8,768]{1,0:T(8,128)(2,1)S(1)} %copy-done, bf16[4,768]{1,0:T(4,128)(2,1)S(1)} %copy-done.3, s32[8,256]{1,0:T(8,128)S(1)} %bitcast.2, s32[8,256]{1,0:T(8,128)S(1)} %bitcast.3, bf16[4096,768]{1,0:T(8,128)(2,1)} %gal_hbm.1), custom_call_target="tpu_custom_call" | custom-call | tf_op jit(solution)/shard_map/pallas_call | solution.py:293
  60.9 0.6 copy.7
Async XLA Ops:
  0.0 0.7 %copy-start = (bf16[8,768]{1,0:T(8,128)(2,1)S(1)}, bf16[8,768]{1,0:T(8,128)(2,1)}, u32[]{:S(2)}) copy-start(bf16[8,768]{1,0:T(8,128)(2,1)} %bankq_ref.1) | copy-start | bytes 36868
  0.7 0.7 %copy-start.1 = (s32[256,8]{0,1:T(8,128)S(1)}, s32[256,8]{0,1:T(8,128)}, u32[]{:S(2)}) copy-start(s32[256,8]{0,1:T(8,128)} %param.8) | copy-start | bytes 24580
  1.4 0.7 %copy-start.2 = (s32[256,8]{0,1:T(8,128)S(1)}, s32[256,8]{0,1:T(8,128)}, u32[]{:S(2)}) copy-start(s32[256,8]{0,1:T(8,128)} %param.9) | copy-start | bytes 24580
  2.1 0.7 %copy-start.3 = (bf16[4,768]{1,0:T(4,128)(2,1)S(1)}, bf16[4,768]{1,0:T(4,128)(2,1)}, u32[]{:S(2)}) copy-start(bf16[4,768]{1,0:T(4,128)(2,1)} %testq_ref.1) | copy-start | bytes 18436

commit v2 on v1

--- a/solution.py
+++ b/solution.py
@@ -23,10 +23,10 @@
 
 def kernel(
     n_bank, n_z, n_y, chunk,
-    bankq_ref, testq_ref, slabs_ref, offsets_ref, gal_hbm,
+    bankq_hbm, testq_hbm, slabs_hbm, offsets_hbm, gal_hbm,
     out_ref,
-    gal, bank_all, test_all, gscale, sums, scores, back_out, back_in,
-    gal_sem, hop_send, hop_recv, sum_send, sum_recv, back_send, back_recv,
+    slabs_ref, offsets_ref, gal, bank_all, test_all, gscale, sums, scores, back_out, back_in,
+    own_sem, gal_sem, hop_send, hop_recv, sum_send, sum_recv, back_send, back_recv,
 ):
     n_gal = n_z * n_y
     rows, width = gal.shape
@@ -41,70 +41,72 @@
         part = pl.ds(n * chunk, chunk)
         return pltpu.make_async_copy(gal_hbm.at[part], gal.at[part], gal_sem.at[n])
 
+    barrier = pltpu.get_barrier_semaphore()
+
+    def far_first(n):
+        return sorted(range(1, n), key=lambda k: -min(k, n - k))
+
+    def ring_peer(axis, k):
+        if axis == 0:
+            return me_z * n_y + (me_y + k) % n_y
+        return (me_z + k) % n_z * n_y + me_y
+
+    for axis, n in ((0, n_y), (1, n_z)):
+        for k in far_first(n):
+            pl.semaphore_signal(
+                barrier, inc=1, device_id={"gal": ring_peer(axis, k)}, device_id_type=MESH
+            )
+    for k in range(1, n_bank):
+        pl.semaphore_signal(
+            barrier, inc=1, device_id={"bank": (me_b + k) % n_bank}, device_id_type=MESH
+        )
+    fetches = [
+        pltpu.make_async_copy(bankq_hbm, bank_all.at[me_z, me_y], own_sem.at[0]),
+        pltpu.make_async_copy(testq_hbm, test_all.at[me_z, me_y], own_sem.at[1]),
+        pltpu.make_async_copy(slabs_hbm, slabs_ref, own_sem.at[2]),
+        pltpu.make_async_copy(offsets_hbm, offsets_ref, own_sem.at[3]),
+    ]
+    for fetch in fetches:
+        fetch.start()
     for n in range(chunks):
         load(n).start()
-
-    barrier = pltpu.get_barrier_semaphore()
-
-    def greet_gal(k, carry):
-        pl.semaphore_signal(
-            barrier, inc=1, device_id={"gal": (me_g + k) % n_gal}, device_id_type=MESH
-        )
-        return carry
-
-    def greet_bank(k, carry):
-        pl.semaphore_signal(
-            barrier, inc=1, device_id={"bank": (me_b + k) % n_bank}, device_id_type=MESH
-        )
-        return carry
-
-    lax.fori_loop(1, n_gal, greet_gal, 0)
-    lax.fori_loop(1, n_bank, greet_bank, 0)
-    pl.semaphore_wait(barrier, n_gal + n_bank - 2)
-
-    gathers = ((bankq_ref, bank_all), (testq_ref, test_all))
+    pl.semaphore_wait(barrier, n_y + n_z + n_bank - 3)
+
+    gathers = ((bankq_hbm, bank_all), (testq_hbm, test_all))
     left, right = pl.ds(0, half), pl.ds(half, half)
 
     def first(t, side, k):
         own, full = gathers[t]
         cols = (left, right)[side]
-        if side == 0:
-            peer = me_z * n_y + (me_y + k) % n_y
-        else:
-            peer = (me_z + k) % n_z * n_y + me_y
         return pltpu.make_async_remote_copy(
             src_ref=own.at[:, cols],
             dst_ref=full.at[me_z, me_y, :, cols],
             send_sem=hop_send.at[t, side, 0, k],
             recv_sem=hop_recv.at[t, side, 0, k],
-            device_id={"gal": peer},
+            device_id={"gal": ring_peer(side, k)},
             device_id_type=MESH,
         )
 
     def second(t, side, k):
         full = gathers[t][1]
         if side == 0:
-            peer = (me_z + k) % n_z * n_y + me_y
             part = full.at[me_z, :, :, left]
         else:
-            peer = me_z * n_y + (me_y + k) % n_y
             part = full.at[:, me_y, :, right]
         return pltpu.make_async_remote_copy(
             src_ref=part,
             dst_ref=part,
             send_sem=hop_send.at[t, side, 1, k],
             recv_sem=hop_recv.at[t, side, 1, k],
-            device_id={"gal": peer},
+            device_id={"gal": ring_peer(1 - side, k)},
             device_id_type=MESH,
         )
 
     spans = ((n_y, n_z), (n_z, n_y))
     for t in range(2):
         for side in range(2):
-            for k in range(1, spans[side][0]):
+            for k in far_first(spans[side][0]):
                 first(t, side, k).start()
-    bank_all[me_z, me_y] = bankq_ref[...]
-    test_all[me_z, me_y] = testq_ref[...]
 
     ones = jnp.ones((8, width), jnp.bfloat16)
 
@@ -119,17 +121,19 @@
         gscale[:, part] = lax.rsqrt(total[0:1] + epsilon)
         return carry
 
-    lax.fori_loop(0, chunks, norms, 0)
-
+    lax.fori_loop(0, chunks, norms, 0, unroll=True)
+
+    for fetch in fetches:
+        fetch.wait()
     for t in range(2):
         for side in range(2):
             for k in range(1, spans[side][0]):
                 first(t, side, k).wait_recv()
-            for k in range(1, spans[side][1]):
+            for k in far_first(spans[side][1]):
                 second(t, side, k).start()
 
     slots = SLOTS * n_gal
-    own_rows = testq_ref.shape[0]
+    own_rows = testq_hbm.shape[0]
     queries = n_gal * own_rows
     slabs = slabs_ref[...]
     offsets = offsets_ref[...].astype(jnp.float32)
@@ -158,7 +162,7 @@
     for side in range(2):
         for k in range(1, spans[side][1]):
             second(0, side, k).wait_recv()
-    portion = bank_all[...].reshape(n_gal * bankq_ref.shape[0], width)
+    portion = bank_all[...].reshape(n_gal * bankq_hbm.shape[0], width)
     values = portion.astype(jnp.float32)
     bank_scale = (SHARPNESS * LOG2E) * lax.rsqrt(
         jnp.sum(values * values, axis=1, keepdims=True) + epsilon
@@ -171,7 +175,7 @@
         sums[me_b, :, part] = jnp.sum(e, axis=0, keepdims=True)
         return carry
 
-    lax.fori_loop(0, chunks, column_sums, 0)
+    lax.fori_loop(0, chunks, column_sums, 0, unroll=True)
 
     def share(k):
         return pltpu.make_async_remote_copy(
@@ -207,7 +211,7 @@
         scores[:, part] = jnp.where(block == slot_block, e, 0.0)
         return carry
 
-    lax.fori_loop(0, chunks, raw_weights, 0)
+    lax.fori_loop(0, chunks, raw_weights, 0, unroll=True)
 
     for k in range(1, n_bank):
         share(k).wait_recv()
@@ -223,7 +227,10 @@
     back_out[...] = message.reshape(n_gal, SLOTS, width + EXTRA)
 
     def give(k, carry):
-        peer = (me_g + k) % n_gal
+        step_z, step_y = k // n_y, k % n_y
+        shift_z = n_z // 2 + jnp.where(step_z % 2 == 1, 1, n_z - 1) * ((step_z + 1) // 2)
+        shift_y = n_y // 2 + jnp.where(step_y % 2 == 1, 1, n_y - 1) * ((step_y + 1) // 2)
+        peer = (me_z + shift_z) % n_z * n_y + (me_y + shift_y) % n_y
         pltpu.make_async_remote_copy(
             src_ref=back_out.at[peer],
             dst_ref=back_in.at[me_g],
@@ -234,7 +241,7 @@
         ).start()
         return carry
 
-    lax.fori_loop(1, n_gal, give, 0)
+    lax.fori_loop(0, n_gal - 1, give, 0)
     back_in[me_g] = back_out[me_g]
 
     slab_of = lax.broadcasted_iota(jnp.int32, (slots, queries), 0) // SLOTS
@@ -293,9 +300,11 @@
     return pl.pallas_call(
         functools.partial(kernel, n_bank, n_z, n_y, chunk),
         out_shape=jax.ShapeDtypeStruct((own_test, width), jnp.float32),
-        in_specs=[vmem] * 4 + [pl.BlockSpec(memory_space=pl.ANY)],
+        in_specs=[pl.BlockSpec(memory_space=pltpu.HBM)] * 5,
         out_specs=vmem,
         scratch_shapes=[
+            pltpu.VMEM(test_slabs.T.shape, jnp.int32),
+            pltpu.VMEM(test_slabs.T.shape, jnp.int32),
             pltpu.VMEM((rows, width), jnp.bfloat16),
             pltpu.VMEM((n_z, n_y, own_bank, width), jnp.bfloat16),
             pltpu.VMEM((n_z, n_y, own_test, width), jnp.bfloat16),
@@ -304,6 +313,7 @@
             pltpu.VMEM((slots, rows), jnp.float32),
             pltpu.VMEM((n_gal, SLOTS, width + EXTRA), jnp.bfloat16),
             pltpu.VMEM((n_gal, SLOTS, width + EXTRA), jnp.bfloat16),
+            pltpu.SemaphoreType.DMA((4,)),
             pltpu.SemaphoreType.DMA((rows // chunk,)),
             pltpu.SemaphoreType.DMA(hops),
             pltpu.SemaphoreType.DMA(hops),
@@ -313,7 +323,7 @@
             pltpu.SemaphoreType.DMA,
         ],
         compiler_params=pltpu.CompilerParams(
-            collective_id=0, has_side_effects=True, vmem_limit_bytes=48 * 1024 * 1024
+            collective_id=0, has_side_effects=True, vmem_limit_bytes=60 * 1024 * 1024
         ),
     )(bank_queries, test_queries, test_slabs.T, test_offsets.T, gallery)
 

time: 61.9 us -> 53.8 us (0.87)
  Pallas kernels: 58.1 us -> 52.3 us
  local copies, waits for them, and re-layouts: 3.39 us -> 1.31 us
    pallas_call x1, Pallas kernels: 58.1 us -> 52.3 us  [body(): pl.pallas_call(functools.partial(kernel, n_bank, n_z, n_y, chunk), out_sh...]
    unnamed x9 -> x1, local copies, waits for them, and re-layouts: 3.39 us -> 1.31 us
where the time goes in v2:
time: 53.8 us; the launch traced here: 53.6 us
  Pallas kernels  52.3 us (97%)
  local copies, waits for them, and re-layouts  1.31 us (2%)
    pallas_call x1, Pallas kernels, body(): pl.pallas_call(functools.partial(kernel, n_bank, n_z, n_y, chunk), out_sh...  52.3 us
    unnamed x1, local copies, waits for them, and re-layouts  1.31 us

profile of v2, /device:TPU:1, one launch (start us, length us, event | category | flops | bytes accessed | tf_op | source)
XLA Modules:
  0.0 53.6 jit_solution(3636372799990946529)
XLA Ops:
  0.0 52.3 %shard_map.55 = f32[4,768]{1,0:T(4,128)} custom-call(bf16[8,768]{1,0:T(8,128)(2,1)} %bankq_hbm.1, bf16[4,768]{1,0:T(4,128)(2,1)} %testq_hbm.1, s32[8,256]{1,0:T(8,128)} %bitcast.2, s32[8,256]{1,0:T(8,128)} %bitcast.3, bf16[4096,768]{1,0:T(8,128)(2,1)} %gal_hbm.1), custom_call_target="tpu_custom_call" | custom-call | tf_op jit(solution)/shard_map/pallas_call | solution.py:300
  52.3 1.3 %copy.7 = f32[4,768]{1,0:T(4,128)} copy(f32[4,768]{1,0:T(4,128)} %shard_map.55) | data formatting | bytes 24576

commit v3 on v2

v3 whole, which is shorter than its diff:
```python
import functools
import jax
import jax.numpy as jnp
from jax import lax
from jax.experimental import pallas as pl
from jax.experimental.pallas import tpu as pltpu
from jax.sharding import PartitionSpec as P

BLOCK = 128
SLOTS = 2
EXTRA = 128
SHARPNESS = 20.0
LOG2E = 1.4426950408889634
epsilon = 1e-06
MESH = pl.DeviceIdType.MESH
NT = (((1,), (1,)), ((), ()))
NN = (((1,), (0,)), ((), ()))


def matmul(left, right, dims):
    return lax.dot_general(left, right, dims, preferred_element_type=jnp.float32)


def kernel(
    n_bank, n_a, n_b, chunk,
    bankq_hbm, testq_hbm, slabs_hbm, offsets_hbm, gal_hbm,
    out_ref,
    slabs_ref, offsets_ref, gal, bank_all, test_row, test_out, test_in,
    gscale, near_sums, sums, scores, back_out, back_in,
    own_sem, gal_sem, bank_send, bank_recv, test_send, test_recv,
    sum_send, sum_recv, back_send, back_recv,
):
    n_gal = n_a * n_b
    rows, width = gal.shape
    chunks = rows // chunk
    me_bank = lax.axis_index("bank")
    me_g = lax.axis_index("gal")
    core = me_bank % 2
    me_a = jnp.where(core == 0, me_g % n_a, me_g // n_b)
    me_b = jnp.where(core == 0, me_g // n_a, me_g % n_b)

    def device(a, b):
        return jnp.where(core == 0, b * n_a + a, a * n_b + b)

    def along_a(k):
        return device((me_a + k) % n_a, me_b)

    def along_b(k):
        return device(me_a, (me_b + k) % n_b)

    def far_first(n):
        return sorted(range(1, n), key=lambda k: -min(k, n - k))

    def load(n):
        part = pl.ds(n * chunk, chunk)
        return pltpu.make_async_copy(gal_hbm.at[part], gal.at[part], gal_sem.at[n])

    barrier = pltpu.get_barrier_semaphore()
    for along, n in ((along_a, n_a), (along_b, n_b)):
        for k in far_first(n):
            pl.semaphore_signal(barrier, inc=1, device_id={"gal": along(k)}, device_id_type=MESH)
    for k in far_first(n_bank):
        pl.semaphore_signal(
            barrier, inc=1, device_id={"bank": (me_bank + k) % n_bank}, device_id_type=MESH
        )
    order = sorted(range(n_b), key=lambda k: (min(k, n_b - k), k))
    place_of = {k: p for p, k in enumerate(order)}
    fetches = [
        pltpu.make_async_copy(bankq_hbm, bank_all.at[0, 0], own_sem.at[0]),
        pltpu.make_async_copy(testq_hbm, test_row.at[me_a], own_sem.at[1]),
        pltpu.make_async_copy(slabs_hbm, slabs_ref, own_sem.at[2]),
        pltpu.make_async_copy(offsets_hbm, offsets_ref, own_sem.at[3]),
    ]
    for fetch in fetches:
        fetch.start()
    for n in range(chunks):
        load(n).start()
    pl.semaphore_wait(barrier, n_a + n_b + n_bank - 3)

    def remote(src, dst, sends, recvs, k, peer):
        return pltpu.make_async_remote_copy(
            src_ref=src,
            dst_ref=dst,
            send_sem=sends.at[k],
            recv_sem=recvs.at[k],
            device_id={"gal": peer},
            device_id_type=MESH,
        )

    def bank_first(k):
        return remote(
            bankq_hbm, bank_all.at[0, n_a - k], bank_send.at[0], bank_recv.at[0], k, along_a(k)
        )

    def test_first(k):
        return remote(
            testq_hbm, test_row.at[me_a], test_send.at[0], test_recv.at[0], k, along_a(k)
        )

    reach = [k for k in far_first(n_b) if min(k, n_b - k) <= 2]

    def bank_second(k):
        return remote(
            bank_all.at[0], bank_all.at[place_of[n_b - k]],
            bank_send.at[1], bank_recv.at[1], k, along_b(k),
        )

    passes = []
    if n_b == 8:
        passes = [(2, 1, 0, n_a, 1), (6, 7, 0, n_a, 7), (2, 2, 0, n_a // 2, 2), (6, 6, n_a // 2, n_a, 6)]

    def bank_third(source, step, low, high, k):
        part = pl.ds(low, high - low)
        return remote(
            bank_all.at[place_of[n_b - source], part],
            bank_all.at[place_of[(2 * n_b - source - step) % n_b], part],
            bank_send.at[2], bank_recv.at[2], k, along_b(step),
        )

    def test_second(k):
        return remote(
            test_out.at[(me_b + k) % n_b], test_in.at[me_b],
            test_send.at[1], test_recv.at[1], k, along_b(k),
        )

    for k in far_first(n_a):
        bank_first(k).start()
    for k in far_first(n_a):
        test_first(k).start()

    ones = jnp.ones((8, width), jnp.bfloat16)

    def norms(n, carry):
        load(n).wait()
        part = pl.ds(pl.multiple_of(n * chunk, chunk), chunk)
        values = gal[part, :].astype(jnp.float32)
        squares = values * values
        high = squares.astype(jnp.bfloat16)
        low = (squares - high.astype(jnp.float32)).astype(jnp.bfloat16)
        total = matmul(ones, high, NT) + matmul(ones, low, NT)
        gscale[:, part] = lax.rsqrt(total[0:1] + epsilon)
        return carry

    lax.fori_loop(0, chunks, norms, 0, unroll=True)

    fetches[0].wait()
    for k in far_first(n_a):
        bank_first(k).wait_recv()
    for k in reach:
        bank_second(k).start()

    for fetch in fetches[1:]:
        fetch.wait()
    slots = SLOTS * n_gal
    own_rows = testq_hbm.shape[0]
    queries = n_gal * own_rows
    slabs = slabs_ref[...]
    offsets = offsets_ref[...].astype(jnp.float32)
    n_list = slabs_ref.shape[0]
    slot_row = lax.broadcasted_iota(jnp.int32, (slots, queries), 0)
    query_col = lax.broadcasted_iota(jnp.int32, (slots, queries), 1)
    row_a = slot_row // SLOTS % n_a
    row_b = slot_row // (SLOTS * n_a)

    def rank_of(hits):
        lane = lax.broadcasted_iota(jnp.int32, hits.shape, 1) % own_rows
        rank = jnp.zeros(hits.shape, jnp.float32)
        for k in range(1, own_rows):
            rank = rank + jnp.where(lane >= k, pltpu.roll(hits, k, 1), 0.0)
        return rank

    target = device(me_a, row_b)
    listed = jnp.zeros((slots, queries), jnp.float32)
    for s in range(n_list):
        listed = listed + jnp.where(slabs[s : s + 1] == target, 1.0, 0.0)
    forward = jnp.where(
        (query_col // own_rows == device(row_a, me_b))
        & (listed > 0.5)
        & (rank_of(listed).astype(jnp.int32) == slot_row % SLOTS),
        1.0,
        0.0,
    )
    ring_row = lax.broadcasted_iota(jnp.int32, (n_a * own_rows, queries), 0)
    ring_col = lax.broadcasted_iota(jnp.int32, (n_a * own_rows, queries), 1)
    fold = jnp.where(
        ring_col == device(ring_row // own_rows, me_b) * own_rows + ring_row % own_rows, 1.0, 0.0
    )
    forward = matmul(forward.astype(jnp.bfloat16), fold.astype(jnp.bfloat16), NT)
    for k in far_first(n_a):
        test_first(k).wait_recv()
    ring_rows = test_row[...].reshape(n_a * own_rows, width)
    packed = matmul(forward.astype(jnp.bfloat16), ring_rows, NN).astype(jnp.bfloat16)
    test_out[...] = packed.reshape(n_b, SLOTS * n_a, width)
    test_in[me_b] = test_out[me_b]

    named = slabs == me_g
    hit = jnp.sum(jnp.where(named, 1.0, 0.0), axis=0, keepdims=True)
    place = jnp.sum(jnp.where(named, offsets, 0.0), axis=0, keepdims=True)
    rank = rank_of(jnp.broadcast_to(hit, (8, queries)))[0:1]
    pick = jnp.where(
        (query_col // own_rows == device(row_a, row_b))
        & (hit > 0.5)
        & (rank.astype(jnp.int32) == slot_row % SLOTS),
        1.0,
        0.0,
    )
    slot_hit = jnp.sum(pick, axis=1, keepdims=True)
    slot_place = jnp.sum(pick * place, axis=1, keepdims=True)
    slot_block = jnp.where(slot_hit > 0.5, slot_place, -1.0).astype(jnp.int32)

    for k in reach:
        bank_second(k).wait_recv()
        for third in passes:
            if third[0] == k:
                bank_third(*third).start()
    for k in far_first(n_b):
        test_second(k).start()

    def column_sums(low, high, write):
        portion = bank_all[low:high].reshape((high - low) * n_a * bankq_hbm.shape[0], width)
        values = portion.astype(jnp.float32)
        bank_scale = (SHARPNESS * LOG2E) * lax.rsqrt(
            jnp.sum(values * values, axis=1, keepdims=True) + epsilon
        )

        def one(n, carry):
            part = pl.ds(pl.multiple_of(n * chunk, chunk), chunk)
            s = matmul(portion, gal[part, :], NT)
            e = jnp.exp2(s * bank_scale * gscale[:, part])
            write(part, jnp.sum(e, axis=0, keepdims=True))
            return carry

        lax.fori_loop(0, chunks, one, 0, unroll=True)

    def near(part, value):
        near_sums[:, part] = value

    def both(part, value):
        sums[me_bank, :, part] = near_sums[:, part] + value

    column_sums(0, n_b // 2, near)
    for third in passes:
        bank_third(*third).wait_recv()
    column_sums(n_b // 2, n_b, both)

    def share(k):
        return pltpu.make_async_remote_copy(
            src_ref=sums.at[me_bank],
            dst_ref=sums.at[me_bank],
            send_sem=sum_send.at[k],
            recv_sem=sum_recv.at[k],
            device_id={"bank": (me_bank + k) % n_bank},
            device_id_type=MESH,
        )

    for k in far_first(n_bank):
        share(k).start()

    for k in far_first(n_b):
        test_second(k).wait_recv()
    packed = test_in[...].reshape(slots, width)
    asked = packed.astype(jnp.float32)
    test_scale = (SHARPNESS * LOG2E) * lax.rsqrt(
        jnp.sum(asked * asked, axis=1, keepdims=True) + epsilon
    )

    def raw_weights(n, carry):
        part = pl.ds(pl.multiple_of(n * chunk, chunk), chunk)
        s = matmul(packed, gal[part, :], NT)
        e = jnp.exp2(s * test_scale * gscale[:, part])
        block = n * (chunk // BLOCK) + (
            lax.broadcasted_iota(jnp.int32, (slots, chunk), 1) // BLOCK
        )
        scores[:, part] = jnp.where(block == slot_block, e, 0.0)
        return carry

    lax.fori_loop(0, chunks, raw_weights, 0, unroll=True)

    for k in range(1, n_bank):
        share(k).wait_recv()
    inverse = 1.0 / jnp.sum(sums[...], axis=0)

    weights = scores[...] * inverse
    total = jnp.sum(weights, axis=1, keepdims=True)
    numer = matmul(weights.astype(jnp.bfloat16), gal[...], NN)
    total_high = total.astype(jnp.bfloat16).astype(jnp.float32)
    lanes = lax.broadcasted_iota(jnp.int32, (slots, EXTRA), 1)
    extra = jnp.where(lanes == 0, total_high, jnp.where(lanes == 1, total - total_high, 0.0))
    message = jnp.concatenate([numer, extra], axis=1).astype(jnp.bfloat16)
    back_out[...] = message.reshape(n_gal, SLOTS, width + EXTRA)

    def give(k, carry):
        step_a, step_b = k // n_b, k % n_b
        shift_a = n_a // 2 + jnp.where(step_a % 2 == 1, 1, n_a - 1) * ((step_a + 1) // 2)
        shift_b = n_b // 2 + jnp.where(step_b % 2 == 1, 1, n_b - 1) * ((step_b + 1) // 2)
        peer_a, peer_b = (me_a + shift_a) % n_a, (me_b + shift_b) % n_b
        pltpu.make_async_remote_copy(
            src_ref=back_out.at[peer_b * n_a + peer_a],
            dst_ref=back_in.at[me_b * n_a + me_a],
            send_sem=back_send,
            recv_sem=back_recv,
            device_id={"gal": device(peer_a, peer_b)},
            device_id_type=MESH,
        ).start()
        return carry

    lax.fori_loop(0, n_gal - 1, give, 0)
    back_in[me_b * n_a + me_a] = back_out[me_b * n_a + me_a]

    slab_of = device(row_a, row_b)
    lists = jnp.zeros((slots, queries), jnp.float32)
    for s in range(n_list):
        lists = lists + jnp.where(slabs[s : s + 1] == slab_of, 1.0, 0.0)
    own_row = lax.broadcasted_iota(jnp.int32, (8, queries), 0)
    own_col = lax.broadcasted_iota(jnp.int32, (8, queries), 1)
    mine = jnp.where(
        (own_col == me_g * own_rows + own_row) & (own_row < own_rows), 1.0, 0.0
    )
    mine_lists = matmul(mine.astype(jnp.bfloat16), lists.astype(jnp.bfloat16), NT)
    before = jnp.where(
        lax.broadcasted_iota(jnp.int32, (8, 8), 1) < lax.broadcasted_iota(jnp.int32, (8, 8), 0),
        1.0,
        0.0,
    )
    mine_rank = matmul(before, mine_lists, NN)
    slot_col = lax.broadcasted_iota(jnp.int32, (8, slots), 1)
    take = jnp.where(
        (mine_lists > 0.5) & ((mine_rank + 0.5).astype(jnp.int32) == slot_col % SLOTS), 1.0, 0.0
    )

    everyone = pltpu.make_async_remote_copy(
        src_ref=back_out.at[pl.ds(0, n_gal - 1)],
        dst_ref=back_in.at[pl.ds(0, n_gal - 1)],
        send_sem=back_send,
        recv_sem=back_recv,
        device_id={"gal": along_a(1)},
        device_id_type=MESH,
    )
    everyone.wait_recv()
    got = back_in[...].reshape(slots, width + EXTRA)
    answer = matmul(take.astype(jnp.bfloat16), got, NN)
    bottom = answer[:, width : width + 1] + answer[:, width + 1 : width + 2]
    out_ref[...] = (answer[:, :width] / bottom)[:own_rows]

    everyone.wait_send()
    for k in range(1, n_bank):
        share(k).wait_send()
    for k in far_first(n_a):
        bank_first(k).wait_send()
        test_first(k).wait_send()
    for k in reach:
        bank_second(k).wait_send()
    for third in passes:
        bank_third(*third).wait_send()
    for k in far_first(n_b):
        test_second(k).wait_send()


def body(n_bank, n_a, n_b, chunk, bank_queries, gallery, test_queries, test_slabs, test_offsets):
    rows, width = gallery.shape
    n_gal = n_a * n_b
    own_bank, own_test = bank_queries.shape[0], test_queries.shape[0]
    slots = SLOTS * n_gal
    vmem = pl.BlockSpec(memory_space=pltpu.VMEM)
    return pl.pallas_call(
        functools.partial(kernel, n_bank, n_a, n_b, chunk),
        out_shape=jax.ShapeDtypeStruct((own_test, width), jnp.float32),
        in_specs=[pl.BlockSpec(memory_space=pltpu.HBM)] * 5,
        out_specs=vmem,
        scratch_shapes=[
            pltpu.VMEM(test_slabs.T.shape, jnp.int32),
            pltpu.VMEM(test_slabs.T.shape, jnp.int32),
            pltpu.VMEM((rows, width), jnp.bfloat16),
            pltpu.VMEM((n_b, n_a, own_bank, width), jnp.bfloat16),
            pltpu.VMEM((n_a, own_test, width), jnp.bfloat16),
            pltpu.VMEM((n_b, SLOTS * n_a, width), jnp.bfloat16),
            pltpu.VMEM((n_b, SLOTS * n_a, width), jnp.bfloat16),
            pltpu.VMEM((1, rows), jnp.float32),
            pltpu.VMEM((1, rows), jnp.float32),
            pltpu.VMEM((n_bank, 1, rows), jnp.float32),
            pltpu.VMEM((slots, rows), jnp.float32),
            pltpu.VMEM((n_gal, SLOTS, width + EXTRA), jnp.bfloat16),
            pltpu.VMEM((n_gal, SLOTS, width + EXTRA), jnp.bfloat16),
            pltpu.SemaphoreType.DMA((4,)),
            pltpu.SemaphoreType.DMA((rows // chunk,)),
            pltpu.SemaphoreType.DMA((3, 8)),
            pltpu.SemaphoreType.DMA((3, 8)),
            pltpu.SemaphoreType.DMA((2, 8)),
            pltpu.SemaphoreType.DMA((2, 8)),
            pltpu.SemaphoreType.DMA((n_bank,)),
            pltpu.SemaphoreType.DMA((n_bank,)),
            pltpu.SemaphoreType.DMA,
            pltpu.SemaphoreType.DMA,
        ],
        compiler_params=pltpu.CompilerParams(
            collective_id=0, has_side_effects=True, vmem_limit_bytes=60 * 1024 * 1024
        ),
    )(bank_queries, test_queries, test_slabs.T, test_offsets.T, gallery)


def solution(mesh):
    n_bank, n_gal = mesh.shape["bank"], mesh.shape["gal"]
    side = int(n_gal**0.5)
    run = functools.partial(body, n_bank, side, side, 512)
    in_specs = (
        P(("bank", "gal"), None),
        P("gal", None),
        P(("bank", "gal"), None),
        P("bank", None),
        P("bank", None),
    )
    out_specs = P(("bank", "gal"), None)
    return jax.shard_map(run, mesh=mesh, in_specs=in_specs, out_specs=out_specs, check_vma=False)
```

time: 53.8 us -> 52.1 us (0.968)
  Pallas kernels: 52.3 us -> 50.6 us
    pallas_call x1, Pallas kernels: 52.3 us -> 50.6 us  [body(): pl.pallas_call(functools.partial(kernel, n_bank, n_a, n_b, chunk), out_sh...]
where the time goes in v3:
time: 52.1 us; the launch traced here: 51.9 us
  Pallas kernels  50.6 us (97%)
  local copies, waits for them, and re-layouts  1.31 us (3%)
    pallas_call x1, Pallas kernels, body(): pl.pallas_call(functools.partial(kernel, n_bank, n_a, n_b, chunk), out_sh...  50.6 us
    unnamed x1, local copies, waits for them, and re-layouts  1.31 us

profile of v3, /device:TPU:1, one launch (start us, length us, event | category | flops | bytes accessed | tf_op | source)
XLA Modules:
  0.0 51.9 jit_solution(9786254798849505525)
XLA Ops:
  0.0 50.6 %shard_map.55 = f32[4,768]{1,0:T(4,128)} custom-call(bf16[8,768]{1,0:T(8,128)(2,1)} %bankq_hbm.1, bf16[4,768]{1,0:T(4,128)(2,1)} %testq_hbm.1, s32[8,256]{1,0:T(8,128)} %bitcast.2, s32[8,256]{1,0:T(8,128)} %bitcast.3, bf16[4096,768]{1,0:T(8,128)(2,1)} %gal_hbm.1), custom_call_target="tpu_custom_call" | custom-call | tf_op jit(solution)/shard_map/pallas_call | solution.py:365
  50.6 1.3 %copy.7 = f32[4,768]{1,0:T(4,128)} copy(f32[4,768]{1,0:T(4,128)} %shard_map.55) | data formatting | bytes 24576

commit v4 on v3

--- a/solution.py
+++ b/solution.py
@@ -73,8 +73,6 @@
     ]
     for fetch in fetches:
         fetch.start()
-    for n in range(chunks):
-        load(n).start()
     pl.semaphore_wait(barrier, n_a + n_b + n_bank - 3)
 
     def remote(src, dst, sends, recvs, k, peer):
@@ -97,7 +95,7 @@
             testq_hbm, test_row.at[me_a], test_send.at[0], test_recv.at[0], k, along_a(k)
         )
 
-    reach = [k for k in far_first(n_b) if min(k, n_b - k) <= 2]
+    reach = [2, 6, 3, 5, 1, 7] if n_b == 8 else far_first(n_b)
 
     def bank_second(k):
         return remote(
@@ -107,7 +105,7 @@
 
     passes = []
     if n_b == 8:
-        passes = [(2, 1, 0, n_a, 1), (6, 7, 0, n_a, 7), (2, 2, 0, n_a // 2, 2), (6, 6, n_a // 2, n_a, 6)]
+        passes = [(2, 2, 0, n_a // 2, 2), (6, 6, n_a // 2, n_a, 6)]
 
     def bank_third(source, step, low, high, k):
         part = pl.ds(low, high - low)
@@ -127,27 +125,8 @@
         bank_first(k).start()
     for k in far_first(n_a):
         test_first(k).start()
-
-    ones = jnp.ones((8, width), jnp.bfloat16)
-
-    def norms(n, carry):
-        load(n).wait()
-        part = pl.ds(pl.multiple_of(n * chunk, chunk), chunk)
-        values = gal[part, :].astype(jnp.float32)
-        squares = values * values
-        high = squares.astype(jnp.bfloat16)
-        low = (squares - high.astype(jnp.float32)).astype(jnp.bfloat16)
-        total = matmul(ones, high, NT) + matmul(ones, low, NT)
-        gscale[:, part] = lax.rsqrt(total[0:1] + epsilon)
-        return carry
-
-    lax.fori_loop(0, chunks, norms, 0, unroll=True)
-
-    fetches[0].wait()
-    for k in far_first(n_a):
-        bank_first(k).wait_recv()
-    for k in reach:
-        bank_second(k).start()
+    for n in range(chunks):
+        load(n).start()
 
     for fetch in fetches[1:]:
         fetch.wait()
@@ -186,12 +165,42 @@
         ring_col == device(ring_row // own_rows, me_b) * own_rows + ring_row % own_rows, 1.0, 0.0
     )
     forward = matmul(forward.astype(jnp.bfloat16), fold.astype(jnp.bfloat16), NT)
+    fetches[0].wait()
+    for k in far_first(n_a):
+        bank_first(k).wait_recv()
+    for k in reach:
+        bank_second(k).start()
+
     for k in far_first(n_a):
         test_first(k).wait_recv()
     ring_rows = test_row[...].reshape(n_a * own_rows, width)
     packed = matmul(forward.astype(jnp.bfloat16), ring_rows, NN).astype(jnp.bfloat16)
     test_out[...] = packed.reshape(n_b, SLOTS * n_a, width)
     test_in[me_b] = test_out[me_b]
+
+
+    ones = jnp.ones((8, width), jnp.bfloat16)
+
+    def norms(n, carry):
+        load(n).wait()
+        part = pl.ds(pl.multiple_of(n * chunk, chunk), chunk)
+        values = gal[part, :].astype(jnp.float32)
+        squares = values * values
+        high = squares.astype(jnp.bfloat16)
+        low = (squares - high.astype(jnp.float32)).astype(jnp.bfloat16)
+        total = matmul(ones, high, NT) + matmul(ones, low, NT)
+        gscale[:, part] = lax.rsqrt(total[0:1] + epsilon)
+        return carry
+
+    lax.fori_loop(0, chunks, norms, 0, unroll=True)
+
+    sources = [third[0] for third in passes]
+    for third in passes:
+        bank_second(third[0]).wait_recv()
+        bank_third(*third).start()
+
+    for k in far_first(n_b):
+        test_second(k).start()
 
     named = slabs == me_g
     hit = jnp.sum(jnp.where(named, 1.0, 0.0), axis=0, keepdims=True)
@@ -208,14 +217,6 @@
     slot_place = jnp.sum(pick * place, axis=1, keepdims=True)
     slot_block = jnp.where(slot_hit > 0.5, slot_place, -1.0).astype(jnp.int32)
 
-    for k in reach:
-        bank_second(k).wait_recv()
-        for third in passes:
-            if third[0] == k:
-                bank_third(*third).start()
-    for k in far_first(n_b):
-        test_second(k).start()
-
     def column_sums(low, high, write):
         portion = bank_all[low:high].reshape((high - low) * n_a * bankq_hbm.shape[0], width)
         values = portion.astype(jnp.float32)
@@ -232,13 +233,20 @@
 
         lax.fori_loop(0, chunks, one, 0, unroll=True)
 
-    def near(part, value):
+    def first_pass(part, value):
         near_sums[:, part] = value
 
     def both(part, value):
         sums[me_bank, :, part] = near_sums[:, part] + value
 
-    column_sums(0, n_b // 2, near)
+    early = [n_b - k for k in order[1 : n_b // 2]]
+    for k in early:
+        if k not in sources:
+            bank_second(k).wait_recv()
+    column_sums(0, n_b // 2, first_pass)
+    for k in reach:
+        if k not in early and k not in sources:
+            bank_second(k).wait_recv()
     for third in passes:
         bank_third(*third).wait_recv()
     column_sums(n_b // 2, n_b, both)
@@ -289,11 +297,12 @@
     message = jnp.concatenate([numer, extra], axis=1).astype(jnp.bfloat16)
     back_out[...] = message.reshape(n_gal, SLOTS, width + EXTRA)
 
-    def give(k, carry):
-        step_a, step_b = k // n_b, k % n_b
-        shift_a = n_a // 2 + jnp.where(step_a % 2 == 1, 1, n_a - 1) * ((step_a + 1) // 2)
-        shift_b = n_b // 2 + jnp.where(step_b % 2 == 1, 1, n_b - 1) * ((step_b + 1) // 2)
-        peer_a, peer_b = (me_a + shift_a) % n_a, (me_b + shift_b) % n_b
+    def near(k, n):
+        return min(k, n - k)
+
+    steps = [(a, b) for a in range(n_a) for b in range(n_b) if (a, b) != (0, 0)]
+    for step_a, step_b in sorted(steps, key=lambda p: -near(p[0], n_a) - near(p[1], n_b)):
+        peer_a, peer_b = (me_a + step_a) % n_a, (me_b + step_b) % n_b
         pltpu.make_async_remote_copy(
             src_ref=back_out.at[peer_b * n_a + peer_a],
             dst_ref=back_in.at[me_b * n_a + me_a],
@@ -302,9 +311,6 @@
             device_id={"gal": device(peer_a, peer_b)},
             device_id_type=MESH,
         ).start()
-        return carry
-
-    lax.fori_loop(0, n_gal - 1, give, 0)
     back_in[me_b * n_a + me_a] = back_out[me_b * n_a + me_a]
 
     slab_of = device(row_a, row_b)

time: 52.1 us -> 50.3 us (0.965)
  Pallas kernels: 50.6 us -> 48.8 us
    pallas_call x1, Pallas kernels: 50.6 us -> 48.8 us  [body(): pl.pallas_call(functools.partial(kernel, n_bank, n_a, n_b, chunk), out_sh...]
where the time goes in v4:
time: 50.3 us; the launch traced here: 50.2 us
  Pallas kernels  48.8 us (97%)
  local copies, waits for them, and re-layouts  1.31 us (3%)
    pallas_call x1, Pallas kernels, body(): pl.pallas_call(functools.partial(kernel, n_bank, n_a, n_b, chunk), out_sh...  48.8 us
    unnamed x1, local copies, waits for them, and re-layouts  1.31 us

profile of v4, /device:TPU:1, one launch (start us, length us, event | category | flops | bytes accessed | tf_op | source)
XLA Modules:
  0.0 50.2 jit_solution(2886931216604000879)
XLA Ops:
  0.0 48.8 %shard_map.55 = f32[4,768]{1,0:T(4,128)} custom-call(bf16[8,768]{1,0:T(8,128)(2,1)} %bankq_hbm.1, bf16[4,768]{1,0:T(4,128)(2,1)} %testq_hbm.1, s32[8,256]{1,0:T(8,128)} %bitcast.2, s32[8,256]{1,0:T(8,128)} %bitcast.3, bf16[4096,768]{1,0:T(8,128)(2,1)} %gal_hbm.1), custom_call_target="tpu_custom_call" | custom-call | tf_op jit(solution)/shard_map/pallas_call | solution.py:371
  48.8 1.3 %copy.7 = f32[4,768]{1,0:T(4,128)} copy(f32[4,768]{1,0:T(4,128)} %shard_map.55) | data formatting | bytes 24576

commit v5 on v4

--- a/solution.py
+++ b/solution.py
@@ -56,13 +56,13 @@
         return pltpu.make_async_copy(gal_hbm.at[part], gal.at[part], gal_sem.at[n])
 
     barrier = pltpu.get_barrier_semaphore()
-    for along, n in ((along_a, n_a), (along_b, n_b)):
-        for k in far_first(n):
-            pl.semaphore_signal(barrier, inc=1, device_id={"gal": along(k)}, device_id_type=MESH)
-    for k in far_first(n_bank):
-        pl.semaphore_signal(
-            barrier, inc=1, device_id={"bank": (me_bank + k) % n_bank}, device_id_type=MESH
-        )
+    greetings = [(min(k, n_a - k), {"gal": along_a(k)}) for k in range(1, n_a)]
+    greetings += [(min(k, n_b - k), {"gal": along_b(k)}) for k in range(1, n_b)]
+    greetings += [
+        (min(k, n_bank - k) // 2, {"bank": (me_bank + k) % n_bank}) for k in range(1, n_bank)
+    ]
+    for _, partner in sorted(greetings, key=lambda g: -g[0]):
+        pl.semaphore_signal(barrier, inc=1, device_id=partner, device_id_type=MESH)
     order = sorted(range(n_b), key=lambda k: (min(k, n_b - k), k))
     place_of = {k: p for p, k in enumerate(order)}
     fetches = [
@@ -90,22 +90,35 @@
             bankq_hbm, bank_all.at[0, n_a - k], bank_send.at[0], bank_recv.at[0], k, along_a(k)
         )
 
+    def bank_early(k):
+        return remote(
+            bankq_hbm, bank_all.at[place_of[n_b - k], 0],
+            bank_send.at[4], bank_recv.at[4], k, along_b(k),
+        )
+
     def test_first(k):
         return remote(
             testq_hbm, test_row.at[me_a], test_send.at[0], test_recv.at[0], k, along_a(k)
         )
 
-    reach = [2, 6, 3, 5, 1, 7] if n_b == 8 else far_first(n_b)
-
-    def bank_second(k):
-        return remote(
-            bank_all.at[0], bank_all.at[place_of[n_b - k]],
-            bank_send.at[1], bank_recv.at[1], k, along_b(k),
+    middle = n_a // 2
+    seconds = [(1, 1, n_a, 1)]
+    if n_b == 8:
+        seconds = [
+            (2, 1, middle, 1), (6, middle, n_a, 1), (3, 1, n_a, 1), (5, 1, n_a, 1),
+            (2, middle, n_a, 3), (6, 1, middle, 3), (1, 1, n_a, 1), (7, 1, n_a, 1),
+        ]
+
+    def bank_second(k, low, high, lot):
+        part = pl.ds(low, high - low)
+        return remote(
+            bank_all.at[0, part], bank_all.at[place_of[n_b - k], part],
+            bank_send.at[lot], bank_recv.at[lot], k, along_b(k),
         )
 
     passes = []
     if n_b == 8:
-        passes = [(2, 2, 0, n_a // 2, 2), (6, 6, n_a // 2, n_a, 6)]
+        passes = [(2, 2, 1, middle, 2), (6, 6, middle, n_a, 6)]
 
     def bank_third(source, step, low, high, k):
         part = pl.ds(low, high - low)
@@ -123,6 +136,8 @@
 
     for k in far_first(n_a):
         bank_first(k).start()
+    for k in far_first(n_b):
+        bank_early(k).start()
     for k in far_first(n_a):
         test_first(k).start()
     for n in range(chunks):
@@ -168,8 +183,8 @@
     fetches[0].wait()
     for k in far_first(n_a):
         bank_first(k).wait_recv()
-    for k in reach:
-        bank_second(k).start()
+    for second in seconds:
+        bank_second(*second).start()
 
     for k in far_first(n_a):
         test_first(k).wait_recv()
@@ -192,15 +207,16 @@
         gscale[:, part] = lax.rsqrt(total[0:1] + epsilon)
         return carry
 
-    lax.fori_loop(0, chunks, norms, 0, unroll=True)
-
-    sources = [third[0] for third in passes]
-    for third in passes:
-        bank_second(third[0]).wait_recv()
+    lax.fori_loop(0, chunks // 2, norms, 0, unroll=True)
+
+    waited = seconds[: len(passes)]
+    for second, third in zip(waited, passes):
+        bank_second(*second).wait_recv()
         bank_third(*third).start()
-
     for k in far_first(n_b):
         test_second(k).start()
+
+    lax.fori_loop(chunks // 2, chunks, norms, 0, unroll=True)
 
     named = slabs == me_g
     hit = jnp.sum(jnp.where(named, 1.0, 0.0), axis=0, keepdims=True)
@@ -231,7 +247,7 @@
             write(part, jnp.sum(e, axis=0, keepdims=True))
             return carry
 
-        lax.fori_loop(0, chunks, one, 0, unroll=True)
+        return one
 
     def first_pass(part, value):
         near_sums[:, part] = value
@@ -239,30 +255,36 @@
     def both(part, value):
         sums[me_bank, :, part] = near_sums[:, part] + value
 
+    for k in far_first(n_b):
+        bank_early(k).wait_recv()
     early = [n_b - k for k in order[1 : n_b // 2]]
-    for k in early:
-        if k not in sources:
-            bank_second(k).wait_recv()
-    column_sums(0, n_b // 2, first_pass)
-    for k in reach:
-        if k not in early and k not in sources:
-            bank_second(k).wait_recv()
+    for second in seconds:
+        if second[0] in early and second not in waited:
+            bank_second(*second).wait_recv()
+    lax.fori_loop(0, chunks, column_sums(0, n_b // 2, first_pass), 0, unroll=True)
+    for second in seconds:
+        if second[0] not in early and second not in waited:
+            bank_second(*second).wait_recv()
     for third in passes:
         bank_third(*third).wait_recv()
-    column_sums(n_b // 2, n_b, both)
-
-    def share(k):
+
+    columns = [pl.ds(h * (rows // 2), rows // 2) for h in range(2)]
+
+    def share(k, h):
         return pltpu.make_async_remote_copy(
-            src_ref=sums.at[me_bank],
-            dst_ref=sums.at[me_bank],
-            send_sem=sum_send.at[k],
-            recv_sem=sum_recv.at[k],
+            src_ref=sums.at[me_bank, :, columns[h]],
+            dst_ref=sums.at[me_bank, :, columns[h]],
+            send_sem=sum_send.at[h, k],
+            recv_sem=sum_recv.at[h, k],
             device_id={"bank": (me_bank + k) % n_bank},
             device_id_type=MESH,
         )
 
-    for k in far_first(n_bank):
-        share(k).start()
+    last_pass = column_sums(n_b // 2, n_b, both)
+    for h in range(2):
+        lax.fori_loop(h * (chunks // 2), (h + 1) * (chunks // 2), last_pass, 0, unroll=True)
+        for k in far_first(n_bank):
+            share(k, h).start()
 
     for k in far_first(n_b):
         test_second(k).wait_recv()
@@ -284,13 +306,15 @@
 
     lax.fori_loop(0, chunks, raw_weights, 0, unroll=True)
 
-    for k in range(1, n_bank):
-        share(k).wait_recv()
-    inverse = 1.0 / jnp.sum(sums[...], axis=0)
-
-    weights = scores[...] * inverse
-    total = jnp.sum(weights, axis=1, keepdims=True)
-    numer = matmul(weights.astype(jnp.bfloat16), gal[...], NN)
+    total = jnp.zeros((slots, 1), jnp.float32)
+    numer = jnp.zeros((slots, width), jnp.float32)
+    for h in range(2):
+        for k in range(1, n_bank):
+            share(k, h).wait_recv()
+        inverse = 1.0 / jnp.sum(sums[:, :, columns[h]], axis=0)
+        weights = scores[:, columns[h]] * inverse
+        total = total + jnp.sum(weights, axis=1, keepdims=True)
+        numer = numer + matmul(weights.astype(jnp.bfloat16), gal[columns[h], :], NN)
     total_high = total.astype(jnp.bfloat16).astype(jnp.float32)
     lanes = lax.broadcasted_iota(jnp.int32, (slots, EXTRA), 1)
     extra = jnp.where(lanes == 0, total_high, jnp.where(lanes == 1, total - total_high, 0.0))
@@ -350,12 +374,15 @@
 
     everyone.wait_send()
     for k in range(1, n_bank):
-        share(k).wait_send()
+        for h in range(2):
+            share(k, h).wait_send()
     for k in far_first(n_a):
         bank_first(k).wait_send()
         test_first(k).wait_send()
-    for k in reach:
-        bank_second(k).wait_send()
+    for k in far_first(n_b):
+        bank_early(k).wait_send()
+    for second in seconds:
+        bank_second(*second).wait_send()
     for third in passes:
         bank_third(*third).wait_send()
     for k in far_first(n_b):
@@ -389,12 +416,12 @@
             pltpu.VMEM((n_gal, SLOTS, width + EXTRA), jnp.bfloat16),
             pltpu.SemaphoreType.DMA((4,)),
             pltpu.SemaphoreType.DMA((rows // chunk,)),
-            pltpu.SemaphoreType.DMA((3, 8)),
-            pltpu.SemaphoreType.DMA((3, 8)),
+            pltpu.SemaphoreType.DMA((5, 8)),
+            pltpu.SemaphoreType.DMA((5, 8)),
             pltpu.SemaphoreType.DMA((2, 8)),
             pltpu.SemaphoreType.DMA((2, 8)),
-            pltpu.SemaphoreType.DMA((n_bank,)),
-            pltpu.SemaphoreType.DMA((n_bank,)),
+            pltpu.SemaphoreType.DMA((2, n_bank)),
+            pltpu.SemaphoreType.DMA((2, n_bank)),
             pltpu.SemaphoreType.DMA,
             pltpu.SemaphoreType.DMA,
         ],

time: 50.3 us -> 49.9 us (level)
  no operation moved by 1% of the time
where the time goes in v5:
time: 49.9 us; the launch traced here: 49.7 us
  Pallas kernels  48.4 us (97%)
  local copies, waits for them, and re-layouts  1.31 us (3%)
    pallas_call x1, Pallas kernels, body(): pl.pallas_call(functools.partial(kernel, n_bank, n_a, n_b, chunk), out_sh...  48.4 us
    unnamed x1, local copies, waits for them, and re-layouts  1.31 us

profile of v5, /device:TPU:1, one launch (start us, length us, event | category | flops | bytes accessed | tf_op | source)
XLA Modules:
  0.0 49.7 jit_solution(8125319417045571752)
XLA Ops:
  0.0 48.4 %shard_map.55 = f32[4,768]{1,0:T(4,128)} custom-call(bf16[8,768]{1,0:T(8,128)(2,1)} %bankq_hbm.1, bf16[4,768]{1,0:T(4,128)(2,1)} %testq_hbm.1, s32[8,256]{1,0:T(8,128)} %bitcast.2, s32[8,256]{1,0:T(8,128)} %bitcast.3, bf16[4096,768]{1,0:T(8,128)(2,1)} %gal_hbm.1), custom_call_target="tpu_custom_call" | custom-call | tf_op jit(solution)/shard_map/pallas_call | solution.py:398
  48.4 1.3 %copy.7 = f32[4,768]{1,0:T(4,128)} copy(f32[4,768]{1,0:T(4,128)} %shard_map.55) | data formatting | bytes 24576

commit v6 on v5

--- a/solution.py
+++ b/solution.py
@@ -268,7 +268,7 @@
     for third in passes:
         bank_third(*third).wait_recv()
 
-    columns = [pl.ds(h * (rows // 2), rows // 2) for h in range(2)]
+    columns = [pl.ds(0, rows)]
 
     def share(k, h):
         return pltpu.make_async_remote_copy(
@@ -281,8 +281,8 @@
         )
 
     last_pass = column_sums(n_b // 2, n_b, both)
-    for h in range(2):
-        lax.fori_loop(h * (chunks // 2), (h + 1) * (chunks // 2), last_pass, 0, unroll=True)
+    for h in range(1):
+        lax.fori_loop(0, chunks, last_pass, 0, unroll=True)
         for k in far_first(n_bank):
             share(k, h).start()
 
@@ -308,7 +308,7 @@
 
     total = jnp.zeros((slots, 1), jnp.float32)
     numer = jnp.zeros((slots, width), jnp.float32)
-    for h in range(2):
+    for h in range(1):
         for k in range(1, n_bank):
             share(k, h).wait_recv()
         inverse = 1.0 / jnp.sum(sums[:, :, columns[h]], axis=0)
@@ -374,7 +374,7 @@
 
     everyone.wait_send()
     for k in range(1, n_bank):
-        for h in range(2):
+        for h in range(1):
             share(k, h).wait_send()
     for k in far_first(n_a):
         bank_first(k).wait_send()

time: 49.9 us -> 49.8 us (level)
  no operation moved by 1% of the time
where the time goes in v6:
time: 49.8 us; the launch traced here: 49.6 us
  Pallas kernels  48.3 us (97%)
  local copies, waits for them, and re-layouts  1.31 us (3%)
    pallas_call x1, Pallas kernels, body(): pl.pallas_call(functools.partial(kernel, n_bank, n_a, n_b, chunk), out_sh...  48.3 us
    unnamed x1, local copies, waits for them, and re-layouts  1.31 us

profile of v6, /device:TPU:1, one launch (start us, length us, event | category | flops | bytes accessed | tf_op | source)
XLA Modules:
  0.0 49.6 jit_solution(8352462101396577782)
XLA Ops:
  0.0 48.3 %shard_map.55 = f32[4,768]{1,0:T(4,128)} custom-call(bf16[8,768]{1,0:T(8,128)(2,1)} %bankq_hbm.1, bf16[4,768]{1,0:T(4,128)(2,1)} %testq_hbm.1, s32[8,256]{1,0:T(8,128)} %bitcast.2, s32[8,256]{1,0:T(8,128)} %bitcast.3, bf16[4096,768]{1,0:T(8,128)(2,1)} %gal_hbm.1), custom_call_target="tpu_custom_call" | custom-call | tf_op jit(solution)/shard_map/pallas_call | solution.py:398
  48.3 1.3 %copy.7 = f32[4,768]{1,0:T(4,128)} copy(f32[4,768]{1,0:T(4,128)} %shard_map.55) | data formatting | bytes 24576
